TPU v7x, 32 devices: a whole 2x2x4 slice. The times are simulated.
32 devices in a mesh: scene: 4 (over y, x), expo: 8 (over z, core).
Axes of the slice: x: 2, y: 2, z: 4, core: 2. Of those that a mesh axis runs over, the one named last changes fastest.
Arguments:
- scene: bfloat16 [2048, 128, 128], P(('scene', 'expo')), may hold values from -6 to 6
- observed: bfloat16 [1024, 128, 128], P('expo'), may hold values from -9 to 9
- inverse_variance: bfloat16 [1024, 128, 128], P('expo'), may hold values from 0.25 to 4
- intersection: int32 [1024, 3], P('expo'), may hold values from 0 to 2047, as said below
- resample_index: int32 [1024, 6], P('expo'), may hold values from 0 to 31
- psf_index: int32 [1024], P('expo'), may hold values from 0 to 15
- resample_bank: bfloat16 [32, 128, 128], replicated, may hold values from -0.5 to 0.5
- psf_bank: bfloat16 [16, 128, 128], replicated, may hold values from -0.5 to 0.5
Outputs:
- gradient: float32 [2048, 128, 128], P(('scene', 'expo'))
Inputs may be any that keep to these rules, and one draw needn't show every extreme that they name: `intersection`: the 3 scene blocks of exposure block j have 3 different owners and lie in sky strips j // 128 - 1 to j // 128 + 1; for each sky strip of exposure blocks, one owner appears in every one of its blocks.
All inputs are finite; a program needn't handle non-finite values.
Results may differ from a plain program's by a relative error of at most 0.014.
Values may be sent and summed in bfloat16 or wider, within the bound.
A program may use at most 128 MiB of HBM per device.

v0:
```python
import jax
import jax.numpy as jnp
from jax import lax
from jax.sharding import PartitionSpec as P


def with_halo(block, sides, width):
    for axis, dim in sides:
        count = lax.axis_size(axis)
        forward = [(i, i + 1) for i in range(count - 1)]
        backward = [(target, source) for source, target in forward]
        low = lax.ppermute(
            lax.slice_in_dim(block, block.shape[dim] - width, None, axis=dim), axis, forward
        )
        high = lax.ppermute(lax.slice_in_dim(block, 0, width, axis=dim), axis, backward)
        block = jnp.concatenate([low, block, high], axis=dim)
    return block


def passed_along(value, axis, steps):
    count = lax.axis_size(axis)
    initial, last = (max(0, -steps), min(count, count - steps))
    return lax.ppermute(value, axis, [(source, source + steps) for source in range(initial, last)])


def psf_pass(resampled, observed, inverse_variance, psf_index, psf_bank):
    blur = psf_bank[psf_index]
    blurred_half = jnp.einsum(
        "jab,jcb->jac", resampled, blur, preferred_element_type=jnp.float32
    ).astype(jnp.bfloat16)
    model = jnp.einsum("jca,jab->jcb", blur, blurred_half, preferred_element_type=jnp.float32)
    weighted = (
        inverse_variance.astype(jnp.float32) * (model - observed.astype(jnp.float32))
    ).astype(jnp.bfloat16)
    back_half = jnp.einsum(
        "jab,jbc->jac", weighted, blur, preferred_element_type=jnp.float32
    ).astype(jnp.bfloat16)
    return jnp.einsum("jba,jbc->jac", blur, back_half, preferred_element_type=jnp.float32).astype(
        jnp.bfloat16
    )


def on_device(
    scene,
    observed,
    inverse_variance,
    intersection,
    resample_index,
    psf_index,
    resample_bank,
    psf_bank,
):
    owner = lax.axis_index("scene")
    strips = lax.axis_size("expo")
    strip = lax.axis_index("expo")
    per_dev = scene.shape[0]
    width = intersection.shape[1]
    near = with_halo(scene, (("expo", 0),), per_dev)
    match = intersection // (strips * per_dev) == owner
    live = jnp.any(match, axis=1)
    column = jnp.argmax(match.astype(jnp.int32), axis=1)
    chosen = jnp.take_along_axis(intersection, column[:, None], axis=1)[:, 0]
    position = (chosen // per_dev % strips - strip + 1) * per_dev + chosen % per_dev
    position = jnp.where(live, jnp.clip(position, 0, 3 * per_dev - 1), 0)
    row_kernel = jnp.take_along_axis(resample_index, column[:, None], axis=1)[:, 0]
    col_kernel = jnp.take_along_axis(resample_index, (column + width)[:, None], axis=1)[:, 0]
    rows = resample_bank[row_kernel]
    cols = resample_bank[col_kernel]
    picked = near[position]
    inner = jnp.einsum("jab,jcb->jac", picked, cols, preferred_element_type=jnp.float32).astype(
        jnp.bfloat16
    )
    term = jnp.einsum("jca,jab->jcb", rows, inner, preferred_element_type=jnp.float32)
    term = jnp.where(live[:, None, None], term, 0.0)
    resampled = lax.psum(term.astype(jnp.bfloat16), "scene")
    adjoint = psf_pass(resampled, observed, inverse_variance, psf_index, psf_bank)
    spread = jnp.einsum("jab,jbc->jac", adjoint, cols, preferred_element_type=jnp.float32).astype(
        jnp.bfloat16
    )
    pulled = jnp.einsum("jba,jbc->jac", rows, spread, preferred_element_type=jnp.float32)
    slots = jnp.arange(3 * per_dev, dtype=jnp.int32)
    selector = ((position[None, :] == slots[:, None]) & live[None, :]).astype(jnp.float32)
    buffer = jnp.einsum("nj,jab->nab", selector, pulled, precision=lax.Precision.HIGHEST)
    lower = buffer[:per_dev]
    middle = buffer[per_dev : 2 * per_dev]
    upper = buffer[2 * per_dev :]
    from_above = passed_along(lower.astype(jnp.bfloat16), "expo", -1).astype(lower.dtype)
    from_below = passed_along(upper.astype(jnp.bfloat16), "expo", 1).astype(upper.dtype)
    return middle + from_above + from_below


def solution(mesh):
    return jax.shard_map(
        on_device,
        mesh=mesh,
        in_specs=(
            P(("scene", "expo"), None, None),
            P("expo", None, None),
            P("expo", None, None),
            P("expo", None),
            P("expo", None),
            P("expo"),
            P(),
            P(),
        ),
        out_specs=P(("scene", "expo"), None, None),
        check_vma=False,
    )
```

profile of v0, /device:TPU:1, one launch (start us, length us, event | category | flops | bytes accessed | tf_op | source)
XLA Modules:
  0.0 259.9 jit_solution(10657741934289266136)
XLA Ops:
  6.5 0.0 copy-start
  6.5 4.7 %collective-permute-start = (bf16[64,128,128]{2,1,0:T(8,128)(2,1)}, bf16[64,128,128]{2,1,0:T(8,128)(2,1)}, u32[]{:S(2)}, u32[]{:S(2)}) collective-permute-start(bf16[64,128,128]{2,1,0:T(8,128)(2,1)} %param.10), channel_id=1, source_target_pairs={{0,1},{1,2},{2,3},{3,4},{4,5},{5,6},{6,7},{8,9},{9,10},{10,11},{11... | collective-permute-start | bytes 6291464 | tf_op jit(solution)/shard_map/ppermute | solution.py:12
  11.3 1.9 collective-permute-start.1
  13.2 0.7 fusion.47
  13.9 0.5 iota_reduce_fusion
  14.5 1.8 gather_fusion.4
  16.3 1.8 gather_fusion.6
  18.1 1.8 gather_fusion.5
  19.9 3.1 %gather_fusion = bf16[128,128,128]{2,1,0:T(8,128)(2,1)} fusion(bf16[32,128,128]{2,1,0:T(8,128)(2,1)S(1)} %copy-done, s32[1024]{0:T(1024)S(1)} %pad_clamp_fusion.3), kind=kCustom, calls=%fused_computation.2 | custom fusion | bytes 8389120 | tf_op jit(solution)/shard_map/gather | solution.py:67
  23.0 3.1 %gather_fusion.3 = bf16[128,128,128]{2,1,0:T(8,128)(2,1)} fusion(bf16[32,128,128]{2,1,0:T(8,128)(2,1)S(1)} %copy-done, s32[1024]{0:T(1024)S(1)} %pad_clamp_fusion), kind=kCustom, calls=%fused_computation.5 | custom fusion | bytes 8389120 | tf_op jit(solution)/shard_map/gather | solution.py:68
  26.1 8.4 %collective-permute-done = bf16[64,128,128]{2,1,0:T(8,128)(2,1)} collective-permute-done((bf16[64,128,128]{2,1,0:T(8,128)(2,1)}, bf16[64,128,128]{2,1,0:T(8,128)(2,1)}, u32[]{:S(2)}, u32[]{:S(2)}) %collective-permute-start) | collective-permute-done | bytes 2097184 | tf_op jit(solution)/shard_map/ppermute | solution.py:12
  34.5 4.4 %collective-permute-done.1 = bf16[64,128,128]{2,1,0:T(8,128)(2,1)} collective-permute-done((bf16[64,128,128]{2,1,0:T(8,128)(2,1)}, bf16[64,128,128]{2,1,0:T(8,128)(2,1)}, u32[]{:S(2)}, u32[]{:S(2)}) %collective-permute-start.1) | collective-permute-done | bytes 2097184 | tf_op jit(solution)/shard_map/ppermute | solution.py:15
  38.9 5.5 %pad_maximum_fusion = bf16[192,128,128]{2,1,0:T(8,128)(2,1)} fusion(bf16[64,128,128]{2,1,0:T(8,128)(2,1)} %collective-permute-done.1, bf16[64,128,128]{2,1,0:T(8,128)(2,1)S(1)} %copy-done.3, bf16[64,128,128]{2,1,0:T(8,128)(2,1)} %collective-permute-done), kind=kLoop, calls=%fused_computation.11 | loop fusion | flops 6291456 | bytes 12582912 | tf_op jit(solution)/shard_map/concatenate | solution.py:16
  44.4 5.9 %gather_fusion.2 = bf16[128,128,128]{2,1,0:T(8,128)(2,1)} fusion(bf16[192,128,128]{2,1,0:T(8,128)(2,1)} %pad_maximum_fusion, s32[1024]{0:T(1024)S(1)} %pad_clamp_fusion.1), kind=kCustom, calls=%fused_computation.4 | custom fusion | bytes 8389120 | tf_op jit(solution)/shard_map/gather | solution.py:69
  50.4 10.8 %select_convert_fusion = bf16[128,128,128]{2,1,0:T(8,128)(2,1)} fusion(pred[128]{0:T(512)(128)(4,1)S(1)} %get-tuple-element.10, bf16[128,128,128]{2,1,0:T(8,128)(2,1)} %gather_fusion, bf16[128,128,128]{2,1,0:T(8,128)(2,1)} %gather_fusion.2, bf16[128,128,128]{2,1,0:T(8,128)(2,1)} %gather_fusion.3), kind=kOutput, calls=%fused_computation.10 | convolution fusion | flops 1080033280 | bytes 16777344 | tf_op jit(solution)/shard_map/jca,jab->jcb/dot_general | solution.py:73
  61.1 0.0 all-reduce.2.cloned.1.call-update
  61.1 0.6 copy-done.4
  61.8 0.4 copy-done.2
  62.2 3.0 %gather_fusion.1 = bf16[128,128,128]{2,1,0:T(8,128)(2,1)} fusion(bf16[16,128,128]{2,1,0:T(8,128)(2,1)S(1)} %copy-done.2, s32[1024]{0:T(1024)S(1)} %pad_clamp_fusion.2), kind=kCustom, calls=%fused_computation.3 | custom fusion | bytes 8389120 | tf_op jit(solution)/shard_map/gather | solution.py:27
  65.2 99.3 %all-reduce.2.cloned.1.call-done = bf16[128,128,128]{2,1,0:T(8,128)(2,1)} async-done(((bf16[128,128,128]{2,1,0:T(8,128)(2,1)}), bf16[128,128,128]{2,1,0:T(8,128)(2,1)}) %all-reduce.2.cloned.1.call-update) | async-done | bytes 4194320 | tf_op jit(solution)/shard_map/psum | solution.py:75
  164.5 8.4 %fusion.51 = bf16[128,128,128]{2,1,0:T(8,128)(2,1)} fusion(bf16[128,128,128]{2,1,0:T(8,128)(2,1)} %all-reduce.2.cloned.1.call-done, bf16[128,128,128]{2,1,0:T(8,128)(2,1)} %gather_fusion.1), kind=kOutput, calls=%fused_computation.86 | convolution fusion | flops 536870912 | bytes 12582912 | tf_op jit(solution)/shard_map/jab,jcb->jac/dot_general | solution.py:28
  172.9 11.8 %fusion.2 = bf16[128,128,128]{2,1,0:T(8,128)(2,1)} fusion(bf16[128,128,128]{2,1,0:T(8,128)(2,1)} %gather_fusion.1, bf16[128,128,128]{2,1,0:T(8,128)(2,1)} %param.11, bf16[128,128,128]{2,1,0:T(8,128)(2,1)} %param.12, bf16[128,128,128]{2,1,0:T(8,128)(2,1)} %fusion.51), kind=kOutput, calls=%fused_computation.12 | convolution fusion | flops 1084227584 | bytes 20971520 | tf_op jit(solution)/shard_map/jab,jbc->jac/dot_general | solution.py:35
  184.7 9.2 %fusion.6 = bf16[128,128,128]{2,1,0:T(8,128)(2,1)} fusion(bf16[128,128,128]{2,1,0:T(8,128)(2,1)} %gather_fusion.3, bf16[128,128,128]{2,1,0:T(8,128)(2,1)} %gather_fusion.1, bf16[128,128,128]{2,1,0:T(8,128)(2,1)} %fusion.2), kind=kOutput, calls=%fused_computation.17 | convolution fusion | flops 1075838976 | bytes 16777216 | tf_op jit(solution)/shard_map/jab,jbc->jac/dot_general | solution.py:77
  193.9 5.2 %fusion.52 = f32[128,128,128]{2,1,0:T(8,128)S(1)} fusion(bf16[128,128,128]{2,1,0:T(8,128)(2,1)} %gather_fusion, bf16[128,128,128]{2,1,0:T(8,128)(2,1)} %fusion.6), kind=kOutput, calls=%fused_computation.87 | convolution fusion | flops 536870912 | bytes 16777216 | tf_op jit(solution)/shard_map/jba,jbc->jac/dot_general | solution.py:80
  199.2 16.3 %fusion.50 = (bf16[192,128,128]{2,0,1:T(8,128)(2,1)S(1)}, f32[192,128,128]{2,0,1:T(8,128)}) fusion(f32[128,128,128]{2,1,0:T(8,128)S(1)} %fusion.52, s32[128]{0:T(128)S(1)} %get-tuple-element.9, pred[128]{0:T(512)(128)(4,1)S(1)} %get-tuple-element.10), kind=kOutput, calls=%fused_computation.85 | convolution fusion | flops 4835033088 | bytes 27263616 | tf_op jit(solution)/shard_map/nj,jab->nab/dot_general | solution.py:83
  215.4 1.0 fusion.49
  216.4 2.8 %collective-permute-start.2 = (bf16[64,128,128]{2,0,1:T(8,128)(2,1)S(1)}, bf16[64,128,128]{2,0,1:T(8,128)(2,1)S(1)}, u32[]{:S(2)}, u32[]{:S(2)}) collective-permute-start(bf16[64,128,128]{2,0,1:T(8,128)(2,1)S(1)} %get-tuple-element.12), channel_id=1, source_target_pairs={{1,0},{2,1},{3,2},{4,3},{5,4},{6,5},{7,6},{9,8},{10,9},{11,10},{12... | collective-permute-start | bytes 6291464 | tf_op jit(solution)/shard_map/ppermute | solution.py:23
  219.2 3.3 %collective-permute-start.3 = (bf16[64,128,128]{2,0,1:T(8,128)(2,1)S(1)}, bf16[64,128,128]{2,0,1:T(8,128)(2,1)S(1)}, u32[]{:S(2)}, u32[]{:S(2)}) collective-permute-start(bf16[64,128,128]{2,0,1:T(8,128)(2,1)S(1)} %get-tuple-element.13), channel_id=1, source_target_pairs={{0,1},{1,2},{2,3},{3,4},{4,5},{5,6},{6,7},{8,9},{9,10},{10,11},{11... | collective-permute-start | bytes 6291464 | tf_op jit(solution)/shard_map/ppermute | solution.py:23
  222.4 21.5 %collective-permute-done.2 = bf16[64,128,128]{2,0,1:T(8,128)(2,1)S(1)} collective-permute-done((bf16[64,128,128]{2,0,1:T(8,128)(2,1)S(1)}, bf16[64,128,128]{2,0,1:T(8,128)(2,1)S(1)}, u32[]{:S(2)}, u32[]{:S(2)}) %collective-permute-start.2) | collective-permute-done | bytes 2097184 | tf_op jit(solution)/shard_map/ppermute | solution.py:23
  243.9 1.2 collective-permute-done.3
  245.1 3.5 %fusion.3 = f32[64,128,128]{2,0,1:T(8,128)S(1)} fusion(f32[192,128,128]{2,0,1:T(8,128)} %get-tuple-element.22, bf16[64,128,128]{2,0,1:T(8,128)(2,1)S(1)} %collective-permute-done.3, bf16[64,128,128]{2,0,1:T(8,128)(2,1)S(1)} %collective-permute-done.2), kind=kLoop, calls=%fused_computation.14 | loop fusion | flops 4194304 | bytes 12582912 | tf_op jit(solution)/shard_map/add | solution.py:89
  248.6 4.4 %copy.10 = f32[64,128,128]{2,1,0:T(8,128)} copy(f32[64,128,128]{2,0,1:T(8,128)S(1)} %fusion.3) | data formatting | bytes 8388608 | tf_op jit(solution)/shard_map/add | solution.py:89
  (21 shorter events, 0.1 us)
Async XLA Ops:
  6.5 13.3 %copy-start = (bf16[32,128,128]{2,1,0:T(8,128)(2,1)S(1)}, bf16[32,128,128]{2,1,0:T(8,128)(2,1)}, u32[]{:S(2)}) copy-start(bf16[32,128,128]{2,1,0:T(8,128)(2,1)} %param.16) | copy-start | bytes 3145732
  6.5 157.9 %all-reduce.2.cloned.1.call-start = ((), (), s32[]{:S(2)}) async-start(), calls=%async_computation | async-start | bytes 8388608 | tf_op jit(solution)/shard_map/psum | solution.py:75
  6.5 28.0 %collective-permute-start = (bf16[64,128,128]{2,1,0:T(8,128)(2,1)}, bf16[64,128,128]{2,1,0:T(8,128)(2,1)}, u32[]{:S(2)}, u32[]{:S(2)}) collective-permute-start(bf16[64,128,128]{2,1,0:T(8,128)(2,1)} %param.10), channel_id=1, source_target_pairs={{0,1},{1,2},{2,3},{3,4},{4,5},{5,6},{6,7},{8,9},{9,10},{10,11},{11... | collective-permute-start | bytes 6291464 | tf_op jit(solution)/shard_map/ppermute | solution.py:12
  11.3 27.7 %collective-permute-start.1 = (bf16[64,128,128]{2,1,0:T(8,128)(2,1)}, bf16[64,128,128]{2,1,0:T(8,128)(2,1)}, u32[]{:S(2)}, u32[]{:S(2)}) collective-permute-start(bf16[64,128,128]{2,1,0:T(8,128)(2,1)} %param.10), channel_id=1, source_target_pairs={{1,0},{2,1},{3,2},{4,3},{5,4},{6,5},{7,6},{9,8},{10,9},{11,10},{12... | collective-permute-start | bytes 6291464 | tf_op jit(solution)/shard_map/ppermute | solution.py:15
  23.0 16.0 %copy-start.3 = (bf16[64,128,128]{2,1,0:T(8,128)(2,1)S(1)}, bf16[64,128,128]{2,1,0:T(8,128)(2,1)}, u32[]{:S(2)}) copy-start(bf16[64,128,128]{2,1,0:T(8,128)(2,1)} %param.10) | copy-start | bytes 6291460
  61.1 0.7 copy-start.4
  61.1 1.1 copy-start.2
  216.4 27.6 %collective-permute-start.2 = (bf16[64,128,128]{2,0,1:T(8,128)(2,1)S(1)}, bf16[64,128,128]{2,0,1:T(8,128)(2,1)S(1)}, u32[]{:S(2)}, u32[]{:S(2)}) collective-permute-start(bf16[64,128,128]{2,0,1:T(8,128)(2,1)S(1)} %get-tuple-element.12), channel_id=1, source_target_pairs={{1,0},{2,1},{3,2},{4,3},{5,4},{6,5},{7,6},{9,8},{10,9},{11,10},{12... | collective-permute-start | bytes 6291464 | tf_op jit(solution)/shard_map/ppermute | solution.py:23
  219.2 26.0 %collective-permute-start.3 = (bf16[64,128,128]{2,0,1:T(8,128)(2,1)S(1)}, bf16[64,128,128]{2,0,1:T(8,128)(2,1)S(1)}, u32[]{:S(2)}, u32[]{:S(2)}) collective-permute-start(bf16[64,128,128]{2,0,1:T(8,128)(2,1)S(1)} %get-tuple-element.13), channel_id=1, source_target_pairs={{0,1},{1,2},{2,3},{3,4},{4,5},{5,6},{6,7},{8,9},{9,10},{10,11},{11... | collective-permute-start | bytes 6291464 | tf_op jit(solution)/shard_map/ppermute | solution.py:23
  245.1 7.9 %copy-start.1 = (bf16[32,128,128]{2,1,0:T(8,128)(2,1)S(1)}, bf16[32,128,128]{2,1,0:T(8,128)(2,1)}, u32[]{:S(2)}) copy-start(bf16[32,128,128]{2,1,0:T(8,128)(2,1)} %param.16) | copy-start | bytes 3145732
Sparse Core Ops, SparseCore 0:
  61.3 103.1 all-reduce.1
where the time goes:
time: 260 us
  waiting for transfers between devices  135 us (52%)
  matrix products  61.7 us (24%)
  local copies, waits for them, and re-layouts  26.9 us (10%)
  between operations  13.5 us (5%)
  starting transfers between devices  12.7 us (5%)
  other arithmetic  10.3 us (4%)
    psum x1, waiting for transfers between devices, on_device(): resampled = lax.psum(term.astype(jnp.bfloat16), 'scene')  99.3 us
    ppermute x2, waiting for transfers between devices, passed_along(): lax.ppermute(value, axis, [(source, source + steps) for source in range(i...  22.7 us
    dot_general x1, matrix products, on_device(): jnp.einsum('nj,jab->nab', selector, pulled, precision=lax.Precision.HIGHEST)  16.3 us
    dot_general x1, matrix products, psf_pass(): jnp.einsum('jab,jbc->jac', weighted, blur, preferred_element_type=jnp.flo...  11.8 us
    dot_general x1, matrix products, on_device(): jnp.einsum('jca,jab->jcb', rows, inner, preferred_element_type=jnp.float32)  10.8 us
    dot_general x1, matrix products, on_device(): jnp.einsum('jab,jbc->jac', adjoint, cols, preferred_element_type=jnp.floa...  9.25 us
    dot_general x1, matrix products, psf_pass(): jnp.einsum('jab,jcb->jac', resampled, blur, preferred_element_type=jnp.fl...  8.44 us
    ppermute x1, waiting for transfers between devices, with_halo(): lax.ppermute(lax.slice_in_dim(block, block.shape[dim] - width, None, axis...  8.41 us
  transfers between devices with their start and end apart: 5, of which 5 were waited for; matrix products, arithmetic and copies ran while one was open for 6% of the time, Pallas kernels for 0%

commit v1 on v0

v1 whole, which is shorter than its diff:
```python
import functools

import jax
import jax.numpy as jnp
from jax import lax
from jax.experimental import pallas as pl
from jax.experimental.pallas import tpu as pltpu
from jax.sharding import PartitionSpec as P

MESH = pl.DeviceIdType.MESH
UNROLL = 4
VMEM_LIMIT = 60 * 1024 * 1024


def dot(a, b, dims):
    return lax.dot_general(a, b, (dims, ((), ())), preferred_element_type=jnp.float32)


NN = ((1,), (0,))
NT = ((1,), (1,))
TN = ((0,), (0,))


def passed_along(value, axis, steps):
    count = lax.axis_size(axis)
    initial, last = (max(0, -steps), min(count, count - steps))
    return lax.ppermute(value, axis, [(source, source + steps) for source in range(initial, last)])


class Plan:
    def __init__(self, owners, exposures):
        self.n = owners
        self.bits = owners.bit_length() - 1
        assert 1 << self.bits == owners
        self.half = exposures // 2
        self.m = self.half // owners
        self.c = min(8, self.m)
        self.chunks = self.m // self.c

    def bit(self, h, p):
        return p if h == 0 else self.bits - 1 - p

    def value(self, owner, h, p):
        return (owner // (1 << self.bit(h, p))) % 2

    def partner(self, owner, h, p):
        step = 1 << self.bit(h, p)
        return owner + step - 2 * step * self.value(owner, h, p)

    def unit(self, owner, h, t):
        u = 0
        for p in range(self.bits):
            weight = self.n >> (p + 1)
            v = self.value(owner, h, p)
            u = u + weight * (v if t & weight else 1 - v)
        return h * self.half + u * self.m

    def base(self, h, t):
        return h * self.half + t * self.m

    def phase(self, t):
        p = 0
        while t >= self.n - (self.n >> (p + 1)):
            p += 1
        return p


def forward_kernel(
    plan, per_dev, pos_s, row_s, col_s, psf_s, scene, observed, weights, bank_h, psf_h, adj,
    near, bank, psf, obs, ivar, terms, got, load_sem, halo_send, halo_recv,
    rs_send, rs_recv, ag_send, ag_recv,
):
    n, m, c = plan.n, plan.m, plan.c
    kernels = bank_h.shape[0]
    owner = lax.axis_index("scene")
    strip = lax.axis_index("expo")
    strips = lax.axis_size("expo")

    barrier = pltpu.get_barrier_semaphore()
    for p in range(plan.bits):
        pl.semaphore_signal(
            barrier, inc=1, device_id={"scene": plan.partner(owner, 0, p)}, device_id_type=MESH
        )

    @pl.when(strip > 0)
    def _():
        pl.semaphore_signal(barrier, inc=1, device_id={"expo": strip - 1}, device_id_type=MESH)

    @pl.when(strip < strips - 1)
    def _():
        pl.semaphore_signal(barrier, inc=1, device_id={"expo": strip + 1}, device_id_type=MESH)

    loads = [
        pltpu.make_async_copy(scene, near.at[pl.ds(per_dev, per_dev)], load_sem.at[0]),
        pltpu.make_async_copy(bank_h, bank.at[pl.ds(0, kernels)], load_sem.at[1]),
        pltpu.make_async_copy(psf_h, psf, load_sem.at[2]),
    ]
    for h in range(2):
        home = plan.unit(owner, h, n - 1)
        loads.append(
            pltpu.make_async_copy(
                observed.at[pl.ds(home, m)], obs.at[pl.ds(h * m, m)], load_sem.at[3 + 2 * h]
            )
        )
        loads.append(
            pltpu.make_async_copy(
                weights.at[pl.ds(home, m)], ivar.at[pl.ds(h * m, m)], load_sem.at[4 + 2 * h]
            )
        )
    for load in loads:
        load.start()
    bank[kernels] = jnp.zeros(bank.shape[1:], bank.dtype)

    below = jnp.where(strip > 0, 1, 0)
    above = jnp.where(strip < strips - 1, 1, 0)
    pl.semaphore_wait(barrier, plan.bits + below + above)

    def halo(k, target):
        return pltpu.make_async_remote_copy(
            src_ref=scene,
            dst_ref=near.at[pl.ds(2 * k * per_dev, per_dev)],
            send_sem=halo_send.at[k],
            recv_sem=halo_recv.at[k],
            device_id={"expo": target},
            device_id_type=MESH,
        )

    @pl.when(strip < strips - 1)
    def _():
        halo(0, strip + 1).start()

    @pl.when(strip > 0)
    def _():
        halo(1, strip - 1).start()

    for load in loads:
        load.wait()

    @pl.when(strip > 0)
    def _():
        halo(0, strip).wait_recv()

    @pl.when(strip < strips - 1)
    def _():
        halo(1, strip).wait_recv()

    def scatter_copy(h, t, k):
        where = plan.base(h, t) + k * c
        slot = where // c
        return pltpu.make_async_remote_copy(
            src_ref=terms.at[pl.ds(where, c)],
            dst_ref=got.at[pl.ds(where, c)],
            send_sem=rs_send.at[slot],
            recv_sem=rs_recv.at[slot],
            device_id={"scene": plan.partner(owner, h, plan.phase(t))},
            device_id_type=MESH,
        )

    def gather_copy(h, t, p, k):
        source = plan.base(h, t) + k * c
        target = plan.base(h, t - (n >> (p + 1))) + k * c
        slot = target // c
        return pltpu.make_async_remote_copy(
            src_ref=adj.at[pl.ds(source, c)],
            dst_ref=adj.at[pl.ds(target, c)],
            send_sem=ag_send.at[slot],
            recv_sem=ag_recv.at[slot],
            device_id={"scene": plan.partner(owner, h, p)},
            device_id_type=MESH,
        )

    def make_terms(h, t, k):
        where = plan.base(h, t) + k * c
        first = plan.unit(owner, h, t) + k * c

        def body(i, carry):
            for e in range(UNROLL):
                j = first + i * UNROLL + e
                block = near[pos_s[j]]
                inner = dot(block, bank[col_s[j]], NT).astype(jnp.bfloat16)
                term = dot(bank[row_s[j]], inner, NN).astype(jnp.bfloat16)
                terms[where + i * UNROLL + e] = term
            return carry

        lax.fori_loop(0, c // UNROLL, body, 0)

    def arrived(t):
        return [t - (n >> (q + 1)) for q in range(plan.bits) if t >= n - (n >> (q + 1))]

    def summed(h, t, k, i):
        total = terms[plan.base(h, t) + k * c + i].astype(jnp.float32)
        for source in arrived(t):
            total = total + got[plan.base(h, source) + k * c + i].astype(jnp.float32)
        return total.astype(jnp.bfloat16)

    def pass_on(h, t, k):
        where = plan.base(h, t) + k * c

        def body(i, carry):
            terms[where + i] = summed(h, t, k, i)
            return carry

        lax.fori_loop(0, c, body, 0)

    def psf_pass(h, k):
        where = plan.base(h, n - 1) + k * c
        first = plan.unit(owner, h, n - 1) + k * c
        here = h * m + k * c

        def body(i, carry):
            for e in range(UNROLL):
                a = i * UNROLL + e
                q = psf[psf_s[first + a]]
                half = dot(summed(h, n - 1, k, a), q, NT).astype(jnp.bfloat16)
                model = dot(q, half, NN)
                weighted = (
                    ivar[here + a].astype(jnp.float32) * (model - obs[here + a].astype(jnp.float32))
                ).astype(jnp.bfloat16)
                back = dot(weighted, q, NN).astype(jnp.bfloat16)
                adj[where + a] = dot(q, back, TN).astype(jnp.bfloat16)
            return carry

        lax.fori_loop(0, c // UNROLL, body, 0)

    for t in range(n):
        for k in range(plan.chunks):
            for h in range(2):
                make_terms(h, t, k)
                if t < n // 2:
                    scatter_copy(h, t, k).start()
    for t in range(n // 2, n):
        for k in range(plan.chunks):
            for h in range(2):
                for source in arrived(t):
                    scatter_copy(h, source, k).wait_recv()
                if t < n - 1:
                    pass_on(h, t, k)
                    scatter_copy(h, t, k).start()
                else:
                    psf_pass(h, k)
                    for p in reversed(range(plan.bits)):
                        gather_copy(h, n - 1, p, k).start()
    for last in reversed(range(plan.bits)):
        for t in range(n - (n >> last), n - (n >> (last + 1))):
            for k in range(plan.chunks):
                for h in range(2):
                    gather_copy(h, t + (n >> (last + 1)), last, k).wait_recv()
                    for p in reversed(range(last)):
                        gather_copy(h, t, p, k).start()
    for t in range(n - 1):
        for k in range(plan.chunks):
            for h in range(2):
                scatter_copy(h, t, k).wait_send()
                p = plan.phase(t)
                gather_copy(h, t + (n >> (p + 1)), p, k).wait_send()

    @pl.when(strip < strips - 1)
    def _():
        halo(0, strip).wait_send()

    @pl.when(strip > 0)
    def _():
        halo(1, strip).wait_send()


def forward(plan, position, row, col, psf_index, scene, observed, weights, bank, psf):
    per_dev = scene.shape[0]
    blocks, side = position.shape[0], scene.shape[1:]
    slots = blocks // plan.c
    dtype = scene.dtype
    smem = pl.BlockSpec(memory_space=pltpu.SMEM)
    hbm = pl.BlockSpec(memory_space=pl.ANY)
    dma = pltpu.SemaphoreType.DMA
    return pl.pallas_call(
        functools.partial(forward_kernel, plan, per_dev),
        out_shape=jax.ShapeDtypeStruct((blocks, *side), dtype),
        in_specs=[smem] * 4 + [hbm] * 5,
        out_specs=pl.BlockSpec(memory_space=pltpu.VMEM),
        scratch_shapes=[
            pltpu.VMEM((3 * per_dev, *side), dtype),
            pltpu.VMEM((bank.shape[0] + 1, *side), dtype),
            pltpu.VMEM(psf.shape, dtype),
            pltpu.VMEM((2 * plan.m, *side), dtype),
            pltpu.VMEM((2 * plan.m, *side), dtype),
            pltpu.VMEM((blocks, *side), dtype),
            pltpu.VMEM((blocks, *side), dtype),
            dma((7,)),
            dma((2,)),
            dma((2,)),
            dma((slots,)),
            dma((slots,)),
            dma((slots,)),
            dma((slots,)),
        ],
        compiler_params=pltpu.CompilerParams(
            collective_id=0, has_side_effects=True, vmem_limit_bytes=VMEM_LIMIT
        ),
        name="forward",
    )(position, row, col, psf_index, scene, observed, weights, bank, psf)


def backward_kernel(
    plan, per_dev, outer, pos_s, row_s, col_s, adj, bank_h, *rest
):
    if outer:
        lower, upper, total, bank, lists, sem = rest
    else:
        total, bank, lists, sem = rest
    kernels = bank_h.shape[0]
    load = pltpu.make_async_copy(bank_h, bank.at[pl.ds(0, kernels)], sem)
    load.start()
    bank[kernels] = jnp.zeros(bank.shape[1:], bank.dtype)

    def clear(i, carry):
        total[i] = jnp.zeros(total.shape[1:], total.dtype)
        return carry

    lax.fori_loop(0, total.shape[0], clear, 0, unroll=2)
    owner = lax.axis_index("scene")
    count = 0
    for h in range(2):
        for t in range(plan.n):
            first, base = plan.unit(owner, h, t), plan.base(h, t)

            def pick(i, count, first=first, base=base):
                position = pos_s[first + i]
                row = row_s[first + i]
                inside = jnp.logical_and(position >= per_dev, position < 2 * per_dev)
                if outer:
                    wanted = jnp.logical_and(row < kernels, jnp.logical_not(inside))
                    slot = jnp.where(position < per_dev, position, position - per_dev)
                else:
                    wanted = jnp.logical_and(row < kernels, inside)
                    slot = position - per_dev
                lists[0, count] = slot
                lists[1, count] = row
                lists[2, count] = col_s[first + i]
                lists[3, count] = base + i
                return count + wanted.astype(jnp.int32)

            count = lax.fori_loop(0, plan.m, pick, count)
    for e in range(UNROLL):
        lists[0, count + e] = 0
        lists[1, count + e] = kernels
        lists[2, count + e] = 0
        lists[3, count + e] = 0
    load.wait()

    def body(i, carry):
        pulled = []
        for e in range(UNROLL):
            a = i * UNROLL + e
            spread = dot(adj[lists[3, a]], bank[lists[2, a]], NN).astype(jnp.bfloat16)
            pulled.append(dot(bank[lists[1, a]], spread, TN))
        for e in range(UNROLL):
            slot = lists[0, i * UNROLL + e]
            total[slot] = total[slot] + pulled[e]
        return carry

    lax.fori_loop(0, (count + UNROLL - 1) // UNROLL, body, 0)
    if outer:

        def put(i, carry):
            lower[i] = total[i].astype(lower.dtype)
            upper[i] = total[per_dev + i].astype(upper.dtype)
            return carry

        lax.fori_loop(0, per_dev, put, 0)


def backward(plan, outer, per_dev, position, row, col, adj, bank):
    side = adj.shape[1:]
    smem = pl.BlockSpec(memory_space=pltpu.SMEM)
    vmem = pl.BlockSpec(memory_space=pltpu.VMEM)
    scratch = [
        pltpu.VMEM((bank.shape[0] + 1, *side), bank.dtype),
        pltpu.SMEM((4, adj.shape[0] + UNROLL), jnp.int32),
        pltpu.SemaphoreType.DMA,
    ]
    if outer:
        shape = [jax.ShapeDtypeStruct((per_dev, *side), jnp.bfloat16)] * 2
        scratch = [pltpu.VMEM((2 * per_dev, *side), jnp.float32)] + scratch
    else:
        shape = jax.ShapeDtypeStruct((per_dev, *side), jnp.float32)
    return pl.pallas_call(
        functools.partial(backward_kernel, plan, per_dev, outer),
        out_shape=shape,
        in_specs=[smem] * 3 + [vmem, pl.BlockSpec(memory_space=pl.ANY)],
        out_specs=[vmem] * 2 if outer else vmem,
        scratch_shapes=scratch,
        compiler_params=pltpu.CompilerParams(vmem_limit_bytes=VMEM_LIMIT // 2),
        cost_estimate=pl.CostEstimate(
            flops=4 * side[0] ** 3 * adj.shape[0] * 4,
            bytes_accessed=adj.size * 4,
            transcendentals=0,
        ),
        name="outer" if outer else "inner",
    )(position, row, col, adj, bank)


def on_device(
    scene,
    observed,
    inverse_variance,
    intersection,
    resample_index,
    psf_index,
    resample_bank,
    psf_bank,
):
    owner = lax.axis_index("scene")
    strips = lax.axis_size("expo")
    strip = lax.axis_index("expo")
    per_dev = scene.shape[0]
    width = intersection.shape[1]
    kernels = resample_bank.shape[0]
    plan = Plan(lax.axis_size("scene"), intersection.shape[0])
    match = intersection // (strips * per_dev) == owner
    live = jnp.any(match, axis=1)
    place = (intersection // per_dev % strips - strip + 1) * per_dev + intersection % per_dev
    place = jnp.clip(place, 0, 3 * per_dev - 1)
    position = jnp.where(live, jnp.sum(jnp.where(match, place, 0), axis=1), per_dev)
    row = jnp.sum(jnp.where(match, resample_index[:, :width], 0), axis=1)
    row = jnp.where(live, row, kernels)
    col = jnp.sum(jnp.where(match, resample_index[:, width:], 0), axis=1)
    adj = forward(
        plan, position, row, col, psf_index, scene, observed, inverse_variance, resample_bank,
        psf_bank,
    )
    lower, upper = backward(plan, True, per_dev, position, row, col, adj, resample_bank)
    from_above = passed_along(lower, "expo", -1)
    from_below = passed_along(upper, "expo", 1)
    middle = backward(plan, False, per_dev, position, row, col, adj, resample_bank)
    return middle + from_above.astype(jnp.float32) + from_below.astype(jnp.float32)


def solution(mesh):
    return jax.shard_map(
        on_device,
        mesh=mesh,
        in_specs=(
            P(("scene", "expo"), None, None),
            P("expo", None, None),
            P("expo", None, None),
            P("expo", None),
            P("expo", None),
            P("expo"),
            P(),
            P(),
        ),
        out_specs=P(("scene", "expo"), None, None),
        check_vma=False,
    )
```

time: 260 us -> 151 us (0.58); the launches traced: 260 us -> 148 us
  waiting for transfers between devices: 135 us -> 17.9 us
  Pallas kernels: 0 us -> 106 us
  matrix products: 61.7 us -> 0 us
  local copies, waits for them, and re-layouts: 26.9 us -> 2.2 us
  between operations: 13.5 us -> 0.09 us
  other arithmetic: 10.3 us -> 4.84 us
  starting transfers between devices: 12.7 us -> 17 us
    pallas_call x0 -> x3, Pallas kernels: none -> 106 us  [the longest x1 93.2 us: forward(): pl.pallas_call(functools.partial(forward_kernel, plan, per_dev), out_shap...]
    psum x1 -> x0, waiting for transfers between devices: 99.3 us -> none  [on_device(): resampled = lax.psum(term.astype(jnp.bfloat16), 'scene')]
    dot_general x6 -> x0, matrix products: 61.7 us -> none  [the longest x1 16.3 us: on_device(): jnp.einsum('nj,jab->nab', selector, pulled, precision=lax.Precision.HIGHEST)]
    gather x7 -> x0, local copies, waits for them, and re-layouts: 20.5 us -> none  [the longest x1 5.93 us: on_device(): picked = near[position]]
    ppermute x2 -> x0, waiting for transfers between devices: 12.8 us -> none  [the longest x1 8.41 us: with_halo(): lax.ppermute(lax.slice_in_dim(block, block.shape[dim] - width, None, axis...]
    ppermute x2, starting transfers between devices: 6.02 us -> 17 us  [passed_along(): lax.ppermute(value, axis, [(source, source + steps) for source in range(i...]
    ppermute x2 -> x0, starting transfers between devices: 6.63 us -> none  [the longest x1 4.71 us: with_halo(): lax.ppermute(lax.slice_in_dim(block, block.shape[dim] - width, None, axis...]
    concatenate x1 -> x0, other arithmetic: 5.5 us -> none  [with_halo(): block = jnp.concatenate([low, block, high], axis=dim)]
  transfers between devices with their start and end apart: 5 -> 2, of which waited for: 5 -> 2; matrix products, arithmetic and copies ran while one was open for 6% -> 0% of each run, Pallas kernels for 0% -> 3%
where the time goes in v1:
time: 151 us; the launch traced here: 148 us
  Pallas kernels  106 us (70%)
  waiting for transfers between devices  17.9 us (12%)
  starting transfers between devices  17 us (11%)
  other arithmetic  4.84 us (3%)
  local copies, waits for them, and re-layouts  2.2 us (1%)
    pallas_call x1, Pallas kernels, forward(): pl.pallas_call(functools.partial(forward_kernel, plan, per_dev), out_shap...  93.2 us
    ppermute x2, waiting for transfers between devices, passed_along(): lax.ppermute(value, axis, [(source, source + steps) for source in range(i...  17.9 us
    ppermute x2, starting transfers between devices, passed_along(): lax.ppermute(value, axis, [(source, source + steps) for source in range(i...  17 us
    pallas_call x2, Pallas kernels, backward(): pl.pallas_call(functools.partial(backward_kernel, plan, per_dev, outer),...  12.9 us
  transfers between devices with their start and end apart: 2, of which 2 were waited for; matrix products, arithmetic and copies ran while one was open for 0% of the time, Pallas kernels for 3%

profile of v1, /device:TPU:1, one launch (start us, length us, event | category | flops | bytes accessed | tf_op | source)
XLA Modules:
  0.0 148.2 jit_solution(18180262508732610333)
XLA Ops:
  0.0 1.3 select_reduce_fusion
  1.3 0.6 broadcast_select_fusion
  1.9 0.0 copy-start.1
  1.9 0.0 copy-start.2
  1.9 0.0 copy-start.3
  1.9 0.0 copy-start.4
  1.9 93.2 %forward.1.adj = bf16[128,128,128]{2,1,0:T(8,128)(2,1)} custom-call(s32[128]{0:T(128)} %get-tuple-element.14.pos_s, s32[128]{0:T(128)} %get-tuple-element.13.row_s, s32[128]{0:T(128)} %get-tuple-element.9.col_s, s32[128]{0:T(128)} %psf_s.1, bf16[64,128,128]{2,1,0:T(8,128)(2,1)} %scene.1, bf16[128,128,128]{2,1,0:T(8,128)(2,1)} %observed.1, ...), custom_call_target="tpu_custom_call" | custom-call | tf_op jit(solution)/shard_map/forward/pallas_call | solution.py:274
  95.1 0.0 copy-done.1
  95.1 0.0 copy-done.2
  95.1 0.0 copy-done.3
  95.1 0.0 copy-done.4
  95.1 0.0 copy-start
  95.2 2.2 %copy-done = bf16[128,128,128]{2,1,0:T(8,128)(2,1)S(1)} copy-done((bf16[128,128,128]{2,1,0:T(8,128)(2,1)S(1)}, bf16[128,128,128]{2,1,0:T(8,128)(2,1)}, u32[]{:S(2)}) %copy-start) | copy-done | bytes 4194328
  97.3 7.9 %outer.1 = (bf16[64,128,128]{2,1,0:T(8,128)(2,1)S(1)}, bf16[64,128,128]{2,1,0:T(8,128)(2,1)S(1)}) custom-call(s32[128]{0:T(128)S(1)} %copy-done.4, s32[128]{0:T(128)S(1)} %copy-done.3, s32[128]{0:T(128)S(1)} %copy-done.2, bf16[128,128,128]{2,1,0:T(8,128)(2,1)S(1)} %copy-done, bf16[32,128,128]{2,1,0:T(8,128)(2,1)S(1)} %copy-done.1), custom_call_target="tpu_custom_call" | custom-call | flops 4294967296 | bytes 8388608 | tf_op jit(solution)/shard_map/outer/pallas_call | solution.py:385
  105.2 1.9 %collective-permute-start = (bf16[64,128,128]{2,1,0:T(8,128)(2,1)S(1)}, bf16[64,128,128]{2,1,0:T(8,128)(2,1)S(1)}, u32[]{:S(2)}, u32[]{:S(2)}) collective-permute-start(bf16[64,128,128]{2,1,0:T(8,128)(2,1)S(1)} %get-tuple-element.7), channel_id=1, source_target_pairs={{1,0},{2,1},{3,2},{4,3},{5,4},{6,5},{7,6},{9,8},{10,9},{11,10},{12... | collective-permute-start | bytes 6291464 | tf_op jit(solution)/shard_map/ppermute | solution.py:27
  107.1 15.1 %collective-permute-start.1 = (bf16[64,128,128]{2,1,0:T(8,128)(2,1)S(1)}, bf16[64,128,128]{2,1,0:T(8,128)(2,1)S(1)}, u32[]{:S(2)}, u32[]{:S(2)}) collective-permute-start(bf16[64,128,128]{2,1,0:T(8,128)(2,1)S(1)} %get-tuple-element.8), channel_id=1, source_target_pairs={{0,1},{1,2},{2,3},{3,4},{4,5},{5,6},{6,7},{8,9},{9,10},{10,11},{11... | collective-permute-start | bytes 6291464 | tf_op jit(solution)/shard_map/ppermute | solution.py:27
  122.2 5.0 %inner.1 = f32[64,128,128]{2,1,0:T(8,128)S(1)} custom-call(s32[128]{0:T(128)S(1)} %copy-done.4, s32[128]{0:T(128)S(1)} %copy-done.3, s32[128]{0:T(128)S(1)} %copy-done.2, bf16[128,128,128]{2,1,0:T(8,128)(2,1)S(1)} %copy-done, bf16[32,128,128]{2,1,0:T(8,128)(2,1)S(1)} %copy-done.1), custom_call_target="tpu_custom_call" | custom-call | flops 4294967296 | bytes 8388608 | tf_op jit(solution)/shard_map/inner/pallas_call | solution.py:385
  127.3 16.8 %collective-permute-done = bf16[64,128,128]{2,1,0:T(8,128)(2,1)S(1)} collective-permute-done((bf16[64,128,128]{2,1,0:T(8,128)(2,1)S(1)}, bf16[64,128,128]{2,1,0:T(8,128)(2,1)S(1)}, u32[]{:S(2)}, u32[]{:S(2)}) %collective-permute-start) | collective-permute-done | bytes 2097184 | tf_op jit(solution)/shard_map/ppermute | solution.py:27
  144.0 1.2 collective-permute-done.1
  145.2 3.0 %convert_add_fusion = f32[64,128,128]{2,1,0:T(8,128)} fusion(bf16[64,128,128]{2,1,0:T(8,128)(2,1)S(1)} %collective-permute-done.1, f32[64,128,128]{2,1,0:T(8,128)S(1)} %inner.1, bf16[64,128,128]{2,1,0:T(8,128)(2,1)S(1)} %collective-permute-done), kind=kLoop, calls=%fused_computation | loop fusion | flops 4194304 | bytes 12582912 | tf_op jit(solution)/shard_map/add | solution.py:434
  (1 shorter events, 0.0 us)
Async XLA Ops:
  1.9 93.2 %copy-start.1 = (bf16[32,128,128]{2,1,0:T(8,128)(2,1)S(1)}, bf16[32,128,128]{2,1,0:T(8,128)(2,1)}, u32[]{:S(2)}) copy-start(bf16[32,128,128]{2,1,0:T(8,128)(2,1)} %bank_h.5) | copy-start | bytes 3145732
  1.9 93.2 %copy-start.2 = (s32[128]{0:T(128)S(1)}, s32[128]{0:T(128)}, u32[]{:S(2)}) copy-start(s32[128]{0:T(128)} %get-tuple-element.9.col_s) | copy-start | bytes 1540
  1.9 93.2 %copy-start.3 = (s32[128]{0:T(128)S(1)}, s32[128]{0:T(128)}, u32[]{:S(2)}) copy-start(s32[128]{0:T(128)} %get-tuple-element.13.row_s) | copy-start | bytes 1540
  1.9 93.3 %copy-start.4 = (s32[128]{0:T(128)S(1)}, s32[128]{0:T(128)}, u32[]{:S(2)}) copy-start(s32[128]{0:T(128)} %get-tuple-element.14.pos_s) | copy-start | bytes 1540
  95.1 2.2 %copy-start = (bf16[128,128,128]{2,1,0:T(8,128)(2,1)S(1)}, bf16[128,128,128]{2,1,0:T(8,128)(2,1)}, u32[]{:S(2)}) copy-start(bf16[128,128,128]{2,1,0:T(8,128)(2,1)} %forward.1.adj) | copy-start | bytes 12582916
  105.2 38.8 %collective-permute-start = (bf16[64,128,128]{2,1,0:T(8,128)(2,1)S(1)}, bf16[64,128,128]{2,1,0:T(8,128)(2,1)S(1)}, u32[]{:S(2)}, u32[]{:S(2)}) collective-permute-start(bf16[64,128,128]{2,1,0:T(8,128)(2,1)S(1)} %get-tuple-element.7), channel_id=1, source_target_pairs={{1,0},{2,1},{3,2},{4,3},{5,4},{6,5},{7,6},{9,8},{10,9},{11,10},{12... | collective-permute-start | bytes 6291464 | tf_op jit(solution)/shard_map/ppermute | solution.py:27
  107.1 38.1 %collective-permute-start.1 = (bf16[64,128,128]{2,1,0:T(8,128)(2,1)S(1)}, bf16[64,128,128]{2,1,0:T(8,128)(2,1)S(1)}, u32[]{:S(2)}, u32[]{:S(2)}) collective-permute-start(bf16[64,128,128]{2,1,0:T(8,128)(2,1)S(1)} %get-tuple-element.8), channel_id=1, source_target_pairs={{0,1},{1,2},{2,3},{3,4},{4,5},{5,6},{6,7},{8,9},{9,10},{10,11},{11... | collective-permute-start | bytes 6291464 | tf_op jit(solution)/shard_map/ppermute | solution.py:27

commit v2 on v1

--- a/solution.py
+++ b/solution.py
@@ -9,6 +9,7 @@
 
 MESH = pl.DeviceIdType.MESH
 UNROLL = 4
+PIECES = 4
 VMEM_LIMIT = 60 * 1024 * 1024
 
 
@@ -19,12 +20,6 @@
 NN = ((1,), (0,))
 NT = ((1,), (1,))
 TN = ((0,), (0,))
-
-
-def passed_along(value, axis, steps):
-    count = lax.axis_size(axis)
-    initial, last = (max(0, -steps), min(count, count - steps))
-    return lax.ppermute(value, axis, [(source, source + steps) for source in range(initial, last)])
 
 
 class Plan:
@@ -58,6 +53,16 @@
     def base(self, h, t):
         return h * self.half + t * self.m
 
+    def turn(self, h, t, k):
+        return (((self.n - 1 - t) * self.chunks + k) * 2 + h) * self.c
+
+    def turns(self, owner, exposures):
+        j = jnp.arange(exposures, dtype=jnp.int32)
+        h, u, i = j // self.half, j % self.half // self.m, j % self.m
+        me = [self.unit(owner, h, self.n - 1) - h * self.half for h in range(2)]
+        apart = jnp.bitwise_xor(u, jnp.where(h == 0, me[0], me[1]) // self.m)
+        return ((apart * self.chunks + i // self.c) * 2 + h) * self.c + i % self.c
+
     def phase(self, t):
         p = 0
         while t >= self.n - (self.n >> (p + 1)):
@@ -66,9 +71,10 @@
 
 
 def forward_kernel(
-    plan, per_dev, pos_s, row_s, col_s, psf_s, scene, observed, weights, bank_h, psf_h, adj,
-    near, bank, psf, obs, ivar, terms, got, load_sem, halo_send, halo_recv,
-    rs_send, rs_recv, ag_send, ag_recv,
+    plan, per_dev, pos_s, row_s, col_s, psf_s, prev_s, last_s, scene, observed, weights, bank_h,
+    psf_h, middle_h, above_h, below_h,
+    near, bank, psf, obs, ivar, terms, got, adj, run, edge, middle, load_sem, halo_send, halo_recv,
+    rs_send, rs_recv, ag_send, ag_recv, lower_send, lower_recv, upper_send, upper_recv, store_sem,
 ):
     n, m, c = plan.n, plan.m, plan.c
     kernels = bank_h.shape[0]
@@ -110,6 +116,7 @@
     for load in loads:
         load.start()
     bank[kernels] = jnp.zeros(bank.shape[1:], bank.dtype)
+    run[0] = jnp.zeros(run.shape[1:], run.dtype)
 
     below = jnp.where(strip > 0, 1, 0)
     above = jnp.where(strip < strips - 1, 1, 0)
@@ -240,13 +247,73 @@
                     psf_pass(h, k)
                     for p in reversed(range(plan.bits)):
                         gather_copy(h, n - 1, p, k).start()
+    def pull(h, t, k):
+        where = plan.base(h, t) + k * c
+        first = plan.unit(owner, h, t) + k * c
+        place = 1 + plan.turn(h, t, k)
+
+        def body(i, carry):
+            pulled = []
+            for e in range(UNROLL):
+                j = first + i * UNROLL + e
+                spread = dot(adj[where + i * UNROLL + e], bank[col_s[j]], NN).astype(jnp.bfloat16)
+                pulled.append(dot(bank[row_s[j]], spread, TN))
+            for e in range(UNROLL):
+                j = first + i * UNROLL + e
+                run[place + i * UNROLL + e] = pulled[e] + run[prev_s[j]]
+            return carry
+
+        lax.fori_loop(0, c // UNROLL, body, 0)
+
+    for k in range(plan.chunks):
+        for h in range(2):
+            pull(h, n - 1, k)
     for last in reversed(range(plan.bits)):
-        for t in range(n - (n >> last), n - (n >> (last + 1))):
+        for t in reversed(range(n - (n >> last), n - (n >> (last + 1)))):
             for k in range(plan.chunks):
                 for h in range(2):
                     gather_copy(h, t + (n >> (last + 1)), last, k).wait_recv()
                     for p in reversed(range(last)):
                         gather_copy(h, t, p, k).start()
+                    pull(h, t, k)
+
+    def edge_copy(up, piece):
+        out, send, recv = (
+            (below_h, upper_send, upper_recv) if up else (above_h, lower_send, lower_recv)
+        )
+        return pltpu.make_async_remote_copy(
+            src_ref=edge.at[pl.ds(up * per_dev + piece * size, size)],
+            dst_ref=out.at[pl.ds(piece * size, size)],
+            send_sem=send.at[piece],
+            recv_sem=recv.at[piece],
+            device_id={"expo": strip + (1 if up else -1)},
+            device_id_type=MESH,
+        )
+
+    pieces = lower_send.shape[0]
+    size = per_dev // pieces
+    for piece in range(pieces):
+        for up in range(2):
+
+            def put(i, carry, up=up, piece=piece):
+                a = piece * size + i
+                edge[up * per_dev + a] = run[last_s[2 * up * per_dev + a]].astype(edge.dtype)
+                return carry
+
+            lax.fori_loop(0, size, put, 0, unroll=2)
+
+            @pl.when(strip < strips - 1 if up else strip > 0)
+            def _(up=up, piece=piece):
+                edge_copy(up, piece).start()
+
+    def own(i, carry):
+        middle[i] = run[last_s[per_dev + i]]
+        return carry
+
+    lax.fori_loop(0, per_dev, own, 0, unroll=2)
+    store = pltpu.make_async_copy(middle, middle_h, store_sem)
+    store.start()
+
     for t in range(n - 1):
         for k in range(plan.chunks):
             for h in range(2):
@@ -257,25 +324,38 @@
     @pl.when(strip < strips - 1)
     def _():
         halo(0, strip).wait_send()
+        for piece in range(pieces):
+            edge_copy(1, piece).wait_send()
+            edge_copy(0, piece).wait_recv()
 
     @pl.when(strip > 0)
     def _():
         halo(1, strip).wait_send()
-
-
-def forward(plan, position, row, col, psf_index, scene, observed, weights, bank, psf):
+        for piece in range(pieces):
+            edge_copy(0, piece).wait_send()
+            edge_copy(1, piece).wait_recv()
+
+    store.wait()
+
+
+def gradient_parts(plan, tables, scene, observed, weights, bank, psf):
     per_dev = scene.shape[0]
-    blocks, side = position.shape[0], scene.shape[1:]
+    blocks, side = tables[0].shape[0], scene.shape[1:]
     slots = blocks // plan.c
+    pieces = PIECES
     dtype = scene.dtype
     smem = pl.BlockSpec(memory_space=pltpu.SMEM)
     hbm = pl.BlockSpec(memory_space=pl.ANY)
     dma = pltpu.SemaphoreType.DMA
     return pl.pallas_call(
         functools.partial(forward_kernel, plan, per_dev),
-        out_shape=jax.ShapeDtypeStruct((blocks, *side), dtype),
-        in_specs=[smem] * 4 + [hbm] * 5,
-        out_specs=pl.BlockSpec(memory_space=pltpu.VMEM),
+        out_shape=[
+            jax.ShapeDtypeStruct((per_dev, *side), jnp.float32),
+            jax.ShapeDtypeStruct((per_dev, *side), jnp.bfloat16),
+            jax.ShapeDtypeStruct((per_dev, *side), jnp.bfloat16),
+        ],
+        in_specs=[smem] * len(tables) + [hbm] * 5,
+        out_specs=[hbm] * 3,
         scratch_shapes=[
             pltpu.VMEM((3 * per_dev, *side), dtype),
             pltpu.VMEM((bank.shape[0] + 1, *side), dtype),
@@ -284,6 +364,10 @@
             pltpu.VMEM((2 * plan.m, *side), dtype),
             pltpu.VMEM((blocks, *side), dtype),
             pltpu.VMEM((blocks, *side), dtype),
+            pltpu.VMEM((blocks, *side), dtype),
+            pltpu.VMEM((blocks + 1, *side), jnp.float32),
+            pltpu.VMEM((2 * per_dev, *side), jnp.bfloat16),
+            pltpu.VMEM((per_dev, *side), jnp.float32),
             dma((7,)),
             dma((2,)),
             dma((2,)),
@@ -291,111 +375,17 @@
             dma((slots,)),
             dma((slots,)),
             dma((slots,)),
+            dma((pieces,)),
+            dma((pieces,)),
+            dma((pieces,)),
+            dma((pieces,)),
+            dma,
         ],
         compiler_params=pltpu.CompilerParams(
             collective_id=0, has_side_effects=True, vmem_limit_bytes=VMEM_LIMIT
         ),
-        name="forward",
-    )(position, row, col, psf_index, scene, observed, weights, bank, psf)
-
-
-def backward_kernel(
-    plan, per_dev, outer, pos_s, row_s, col_s, adj, bank_h, *rest
-):
-    if outer:
-        lower, upper, total, bank, lists, sem = rest
-    else:
-        total, bank, lists, sem = rest
-    kernels = bank_h.shape[0]
-    load = pltpu.make_async_copy(bank_h, bank.at[pl.ds(0, kernels)], sem)
-    load.start()
-    bank[kernels] = jnp.zeros(bank.shape[1:], bank.dtype)
-
-    def clear(i, carry):
-        total[i] = jnp.zeros(total.shape[1:], total.dtype)
-        return carry
-
-    lax.fori_loop(0, total.shape[0], clear, 0, unroll=2)
-    owner = lax.axis_index("scene")
-    count = 0
-    for h in range(2):
-        for t in range(plan.n):
-            first, base = plan.unit(owner, h, t), plan.base(h, t)
-
-            def pick(i, count, first=first, base=base):
-                position = pos_s[first + i]
-                row = row_s[first + i]
-                inside = jnp.logical_and(position >= per_dev, position < 2 * per_dev)
-                if outer:
-                    wanted = jnp.logical_and(row < kernels, jnp.logical_not(inside))
-                    slot = jnp.where(position < per_dev, position, position - per_dev)
-                else:
-                    wanted = jnp.logical_and(row < kernels, inside)
-                    slot = position - per_dev
-                lists[0, count] = slot
-                lists[1, count] = row
-                lists[2, count] = col_s[first + i]
-                lists[3, count] = base + i
-                return count + wanted.astype(jnp.int32)
-
-            count = lax.fori_loop(0, plan.m, pick, count)
-    for e in range(UNROLL):
-        lists[0, count + e] = 0
-        lists[1, count + e] = kernels
-        lists[2, count + e] = 0
-        lists[3, count + e] = 0
-    load.wait()
-
-    def body(i, carry):
-        pulled = []
-        for e in range(UNROLL):
-            a = i * UNROLL + e
-            spread = dot(adj[lists[3, a]], bank[lists[2, a]], NN).astype(jnp.bfloat16)
-            pulled.append(dot(bank[lists[1, a]], spread, TN))
-        for e in range(UNROLL):
-            slot = lists[0, i * UNROLL + e]
-            total[slot] = total[slot] + pulled[e]
-        return carry
-
-    lax.fori_loop(0, (count + UNROLL - 1) // UNROLL, body, 0)
-    if outer:
-
-        def put(i, carry):
-            lower[i] = total[i].astype(lower.dtype)
-            upper[i] = total[per_dev + i].astype(upper.dtype)
-            return carry
-
-        lax.fori_loop(0, per_dev, put, 0)
-
-
-def backward(plan, outer, per_dev, position, row, col, adj, bank):
-    side = adj.shape[1:]
-    smem = pl.BlockSpec(memory_space=pltpu.SMEM)
-    vmem = pl.BlockSpec(memory_space=pltpu.VMEM)
-    scratch = [
-        pltpu.VMEM((bank.shape[0] + 1, *side), bank.dtype),
-        pltpu.SMEM((4, adj.shape[0] + UNROLL), jnp.int32),
-        pltpu.SemaphoreType.DMA,
-    ]
-    if outer:
-        shape = [jax.ShapeDtypeStruct((per_dev, *side), jnp.bfloat16)] * 2
-        scratch = [pltpu.VMEM((2 * per_dev, *side), jnp.float32)] + scratch
-    else:
-        shape = jax.ShapeDtypeStruct((per_dev, *side), jnp.float32)
-    return pl.pallas_call(
-        functools.partial(backward_kernel, plan, per_dev, outer),
-        out_shape=shape,
-        in_specs=[smem] * 3 + [vmem, pl.BlockSpec(memory_space=pl.ANY)],
-        out_specs=[vmem] * 2 if outer else vmem,
-        scratch_shapes=scratch,
-        compiler_params=pltpu.CompilerParams(vmem_limit_bytes=VMEM_LIMIT // 2),
-        cost_estimate=pl.CostEstimate(
-            flops=4 * side[0] ** 3 * adj.shape[0] * 4,
-            bytes_accessed=adj.size * 4,
-            transcendentals=0,
-        ),
-        name="outer" if outer else "inner",
-    )(position, row, col, adj, bank)
+        name="gradient",
+    )(*tables, scene, observed, weights, bank, psf)
 
 
 def on_device(
@@ -423,15 +413,19 @@
     row = jnp.sum(jnp.where(match, resample_index[:, :width], 0), axis=1)
     row = jnp.where(live, row, kernels)
     col = jnp.sum(jnp.where(match, resample_index[:, width:], 0), axis=1)
-    adj = forward(
-        plan, position, row, col, psf_index, scene, observed, inverse_variance, resample_bank,
-        psf_bank,
+    slot = jnp.where(live, position, -1)
+    turn = plan.turns(owner, slot.shape[0])
+    before = (slot[:, None] == slot[None, :]) & (turn[None, :] < turn[:, None])
+    prev = jnp.max(jnp.where(before, turn[None, :] + 1, 0), axis=1)
+    slots = jnp.arange(3 * per_dev, dtype=jnp.int32)
+    last = jnp.max(jnp.where(slots[:, None] == slot[None, :], turn[None, :] + 1, 0), axis=1)
+    middle, above, below = gradient_parts(
+        plan, (position, row, col, psf_index, prev, last), scene, observed, inverse_variance,
+        resample_bank, psf_bank,
     )
-    lower, upper = backward(plan, True, per_dev, position, row, col, adj, resample_bank)
-    from_above = passed_along(lower, "expo", -1)
-    from_below = passed_along(upper, "expo", 1)
-    middle = backward(plan, False, per_dev, position, row, col, adj, resample_bank)
-    return middle + from_above.astype(jnp.float32) + from_below.astype(jnp.float32)
+    above = jnp.where(strip < strips - 1, above.astype(jnp.float32), 0.0)
+    below = jnp.where(strip > 0, below.astype(jnp.float32), 0.0)
+    return middle + above + below
 
 
 def solution(mesh):

time: 151 us -> 140 us (0.927); the launches traced: 148 us -> 139 us
  Pallas kernels: 106 us -> 129 us
  waiting for transfers between devices: 17.9 us -> 0 us
  starting transfers between devices: 17 us -> 0 us
  other arithmetic: 4.84 us -> 9.89 us
  local copies, waits for them, and re-layouts: 2.2 us -> 0 us
    pallas_call x3 -> x1, Pallas kernels: 106 us -> 129 us  [gradient_parts(): pl.pallas_call(functools.partial(forward_kernel, plan, per_dev), out_shap...]
    ppermute x2 -> x0, waiting for transfers between devices: 17.9 us -> none  [passed_along(): lax.ppermute(value, axis, [(source, source + steps) for source in range(i...]
    ppermute x2 -> x0, starting transfers between devices: 17 us -> none  [passed_along(): lax.ppermute(value, axis, [(source, source + steps) for source in range(i...]
    add x1 -> x2, other arithmetic: 2.96 us -> 7.21 us  [the longest x1 6.68 us: on_device(): return middle + above + below]
    unnamed x10 -> x0, local copies, waits for them, and re-layouts: 2.2 us -> none
  transfers between devices with their start and end apart: 2 -> 0, of which waited for: 2 -> 0; matrix products, arithmetic and copies ran while one was open for 0% -> 0% of each run, Pallas kernels for 3% -> 0%
where the time goes in v2:
time: 140 us; the launch traced here: 139 us
  Pallas kernels  129 us (92%)
  other arithmetic  9.89 us (7%)
    pallas_call x1, Pallas kernels, gradient_parts(): pl.pallas_call(functools.partial(forward_kernel, plan, per_dev), out_shap...  129 us
    add x1, other arithmetic, on_device(): return middle + above + below  6.68 us

profile of v2, /device:TPU:1, one launch (start us, length us, event | category | flops | bytes accessed | tf_op | source)
XLA Modules:
  0.0 139.3 jit_solution(112975397457892663)
XLA Ops:
  0.0 1.3 select_reduce_fusion.2
  1.3 0.5 broadcast_add_fusion
  1.8 0.7 select_reduce_fusion.1.prev_s
  2.5 0.7 select_reduce_fusion.last_s
  3.2 129.4 %gradient.1 = (f32[64,128,128]{2,1,0:T(8,128)}, bf16[64,128,128]{2,1,0:T(8,128)(2,1)}, bf16[64,128,128]{2,1,0:T(8,128)(2,1)}) custom-call(s32[128]{0:T(128)} %get-tuple-element.21.pos_s, s32[128]{0:T(128)} %get-tuple-element.20.row_s, s32[128]{0:T(128)} %get-tuple-element.11.col_s, s32[128]{0:T(128)} %psf_s.1, s32[128]{0:T(128)} %select_reduce_fusion.1.prev_s, ...), custom_call_target="tpu_custom_call" | custom-call | tf_op jit(solution)/shard_map/gradient/pallas_call | solution.py:350
  132.6 6.7 %select_add_fusion = f32[64,128,128]{2,1,0:T(8,128)} fusion(bf16[64,128,128]{2,1,0:T(8,128)(2,1)} %get-tuple-element.10, f32[64,128,128]{2,1,0:T(8,128)} %get-tuple-element.8, bf16[64,128,128]{2,1,0:T(8,128)(2,1)} %get-tuple-element.9, pred[]{:T(512)S(6)} %gt.3, pred[]{:T(512)S(6)} %lt.66), kind=kLoop, calls=%fused_computation | loop fusion | flops 6291456 | bytes 12582914 | tf_op jit(solution)/shard_map/add | solution.py:428
  (1 shorter events, 0.0 us)

commit v3 on v2

--- a/solution.py
+++ b/solution.py
@@ -10,7 +10,7 @@
 MESH = pl.DeviceIdType.MESH
 UNROLL = 4
 PIECES = 4
-VMEM_LIMIT = 60 * 1024 * 1024
+VMEM_LIMIT = 50 * 1024 * 1024
 
 
 def dot(a, b, dims):
@@ -20,6 +20,12 @@
 NN = ((1,), (0,))
 NT = ((1,), (1,))
 TN = ((0,), (0,))
+
+
+def passed_along(value, axis, steps):
+    count = lax.axis_size(axis)
+    initial, last = (max(0, -steps), min(count, count - steps))
+    return lax.ppermute(value, axis, [(source, source + steps) for source in range(initial, last)])
 
 
 class Plan:
@@ -71,9 +77,9 @@
 
 
 def forward_kernel(
-    plan, per_dev, pos_s, row_s, col_s, psf_s, prev_s, last_s, scene, observed, weights, bank_h,
+    plan, per_dev, pos_s, own_s, give_s, row_s, col_s, psf_s, prev_s, last_s, scene, observed, weights, bank_h,
     psf_h, middle_h, above_h, below_h,
-    near, bank, psf, obs, ivar, terms, got, adj, run, edge, middle, load_sem, halo_send, halo_recv,
+    held, stage, came, bank, psf, obs, ivar, terms, got, adj, run, middle, load_sem, z_send, z_recv,
     rs_send, rs_recv, ag_send, ag_recv, lower_send, lower_recv, upper_send, upper_recv, store_sem,
 ):
     n, m, c = plan.n, plan.m, plan.c
@@ -97,7 +103,7 @@
         pl.semaphore_signal(barrier, inc=1, device_id={"expo": strip + 1}, device_id_type=MESH)
 
     loads = [
-        pltpu.make_async_copy(scene, near.at[pl.ds(per_dev, per_dev)], load_sem.at[0]),
+        pltpu.make_async_copy(scene, held, load_sem.at[0]),
         pltpu.make_async_copy(bank_h, bank.at[pl.ds(0, kernels)], load_sem.at[1]),
         pltpu.make_async_copy(psf_h, psf, load_sem.at[2]),
     ]
@@ -122,34 +128,55 @@
     above = jnp.where(strip < strips - 1, 1, 0)
     pl.semaphore_wait(barrier, plan.bits + below + above)
 
-    def halo(k, target):
+    blocks = terms.shape[0]
+
+    def z_copy(up, h, t, k):
+        where = (0 if up else blocks) + plan.base(h, t) + k * c
         return pltpu.make_async_remote_copy(
-            src_ref=scene,
-            dst_ref=near.at[pl.ds(2 * k * per_dev, per_dev)],
-            send_sem=halo_send.at[k],
-            recv_sem=halo_recv.at[k],
-            device_id={"expo": target},
+            src_ref=stage.at[pl.ds(where, c)],
+            dst_ref=came.at[pl.ds(where, c)],
+            send_sem=z_send.at[where // c],
+            recv_sem=z_recv.at[where // c],
+            device_id={"expo": strip + (1 if up else -1)},
             device_id_type=MESH,
         )
 
-    @pl.when(strip < strips - 1)
-    def _():
-        halo(0, strip + 1).start()
-
-    @pl.when(strip > 0)
-    def _():
-        halo(1, strip - 1).start()
-
-    for load in loads:
+    loads[0].wait()
+    for t in range(n):
+        for k in range(plan.chunks):
+            for h in range(2):
+                for up in (1, 0):
+                    first = (0 if up else blocks) + plan.unit(owner, h, t) + k * c
+                    where = (0 if up else blocks) + plan.base(h, t) + k * c
+
+                    def fill(i, carry, first=first, where=where):
+                        stage[where + i] = held[give_s[first + i]]
+                        return carry
+
+                    lax.fori_loop(0, c, fill, 0, unroll=2)
+
+                    @pl.when(strip < strips - 1 if up else strip > 0)
+                    def _(up=up, h=h, t=t, k=k):
+                        z_copy(up, h, t, k).start()
+
+    @pl.when(strip == 0)
+    def _():
+        def wipe(i, carry):
+            came[i] = jnp.zeros(came.shape[1:], came.dtype)
+            return carry
+
+        lax.fori_loop(0, blocks, wipe, 0)
+
+    @pl.when(strip == strips - 1)
+    def _():
+        def wipe(i, carry):
+            came[blocks + i] = jnp.zeros(came.shape[1:], came.dtype)
+            return carry
+
+        lax.fori_loop(0, blocks, wipe, 0)
+
+    for load in loads[1:]:
         load.wait()
-
-    @pl.when(strip > 0)
-    def _():
-        halo(0, strip).wait_recv()
-
-    @pl.when(strip < strips - 1)
-    def _():
-        halo(1, strip).wait_recv()
 
     def scatter_copy(h, t, k):
         where = plan.base(h, t) + k * c
@@ -183,7 +210,10 @@
         def body(i, carry):
             for e in range(UNROLL):
                 j = first + i * UNROLL + e
-                block = near[pos_s[j]]
+                position = pos_s[j]
+                here = where + i * UNROLL + e
+                block = lax.select(position < per_dev, came[here], held[own_s[j]])
+                block = lax.select(position >= 2 * per_dev, came[blocks + here], block)
                 inner = dot(block, bank[col_s[j]], NT).astype(jnp.bfloat16)
                 term = dot(bank[row_s[j]], inner, NN).astype(jnp.bfloat16)
                 terms[where + i * UNROLL + e] = term
@@ -232,21 +262,40 @@
     for t in range(n):
         for k in range(plan.chunks):
             for h in range(2):
+
+                @pl.when(strip > 0)
+                def _(h=h, t=t, k=k):
+                    z_copy(1, h, t, k).wait_recv()
+
+                @pl.when(strip < strips - 1)
+                def _(h=h, t=t, k=k):
+                    z_copy(0, h, t, k).wait_recv()
+
                 make_terms(h, t, k)
+                for source in arrived(t):
+                    scatter_copy(h, source, k).wait_recv()
                 if t < n // 2:
                     scatter_copy(h, t, k).start()
-    for t in range(n // 2, n):
-        for k in range(plan.chunks):
-            for h in range(2):
-                for source in arrived(t):
-                    scatter_copy(h, source, k).wait_recv()
-                if t < n - 1:
+                elif t < n - 1:
                     pass_on(h, t, k)
                     scatter_copy(h, t, k).start()
                 else:
                     psf_pass(h, k)
                     for p in reversed(range(plan.bits)):
                         gather_copy(h, n - 1, p, k).start()
+
+    for t in range(n):
+        for k in range(plan.chunks):
+            for h in range(2):
+
+                @pl.when(strip < strips - 1)
+                def _(h=h, t=t, k=k):
+                    z_copy(1, h, t, k).wait_send()
+
+                @pl.when(strip > 0)
+                def _(h=h, t=t, k=k):
+                    z_copy(0, h, t, k).wait_send()
+
     def pull(h, t, k):
         where = plan.base(h, t) + k * c
         first = plan.unit(owner, h, t) + k * c
@@ -282,7 +331,7 @@
             (below_h, upper_send, upper_recv) if up else (above_h, lower_send, lower_recv)
         )
         return pltpu.make_async_remote_copy(
-            src_ref=edge.at[pl.ds(up * per_dev + piece * size, size)],
+            src_ref=stage.at[pl.ds(up * per_dev + piece * size, size)],
             dst_ref=out.at[pl.ds(piece * size, size)],
             send_sem=send.at[piece],
             recv_sem=recv.at[piece],
@@ -297,7 +346,7 @@
 
             def put(i, carry, up=up, piece=piece):
                 a = piece * size + i
-                edge[up * per_dev + a] = run[last_s[2 * up * per_dev + a]].astype(edge.dtype)
+                stage[up * per_dev + a] = run[last_s[2 * up * per_dev + a]].astype(stage.dtype)
                 return carry
 
             lax.fori_loop(0, size, put, 0, unroll=2)
@@ -323,14 +372,12 @@
 
     @pl.when(strip < strips - 1)
     def _():
-        halo(0, strip).wait_send()
         for piece in range(pieces):
             edge_copy(1, piece).wait_send()
             edge_copy(0, piece).wait_recv()
 
     @pl.when(strip > 0)
     def _():
-        halo(1, strip).wait_send()
         for piece in range(pieces):
             edge_copy(0, piece).wait_send()
             edge_copy(1, piece).wait_recv()
@@ -357,7 +404,9 @@
         in_specs=[smem] * len(tables) + [hbm] * 5,
         out_specs=[hbm] * 3,
         scratch_shapes=[
-            pltpu.VMEM((3 * per_dev, *side), dtype),
+            pltpu.VMEM((per_dev, *side), dtype),
+            pltpu.VMEM((2 * blocks, *side), dtype),
+            pltpu.VMEM((2 * blocks, *side), dtype),
             pltpu.VMEM((bank.shape[0] + 1, *side), dtype),
             pltpu.VMEM(psf.shape, dtype),
             pltpu.VMEM((2 * plan.m, *side), dtype),
@@ -366,11 +415,10 @@
             pltpu.VMEM((blocks, *side), dtype),
             pltpu.VMEM((blocks, *side), dtype),
             pltpu.VMEM((blocks + 1, *side), jnp.float32),
-            pltpu.VMEM((2 * per_dev, *side), jnp.bfloat16),
             pltpu.VMEM((per_dev, *side), jnp.float32),
             dma((7,)),
-            dma((2,)),
-            dma((2,)),
+            dma((2 * slots,)),
+            dma((2 * slots,)),
             dma((slots,)),
             dma((slots,)),
             dma((slots,)),
@@ -413,6 +461,10 @@
     row = jnp.sum(jnp.where(match, resample_index[:, :width], 0), axis=1)
     row = jnp.where(live, row, kernels)
     col = jnp.sum(jnp.where(match, resample_index[:, width:], 0), axis=1)
+    own = jnp.clip(position - per_dev, 0, per_dev - 1)
+    low = jnp.where(position < per_dev, position, 0)
+    high = jnp.maximum(position - 2 * per_dev, 0)
+    give = jnp.concatenate([passed_along(low, "expo", -1), passed_along(high, "expo", 1)])
     slot = jnp.where(live, position, -1)
     turn = plan.turns(owner, slot.shape[0])
     before = (slot[:, None] == slot[None, :]) & (turn[None, :] < turn[:, None])
@@ -420,7 +472,7 @@
     slots = jnp.arange(3 * per_dev, dtype=jnp.int32)
     last = jnp.max(jnp.where(slots[:, None] == slot[None, :], turn[None, :] + 1, 0), axis=1)
     middle, above, below = gradient_parts(
-        plan, (position, row, col, psf_index, prev, last), scene, observed, inverse_variance,
+        plan, (position, own, give, row, col, psf_index, prev, last), scene, observed, inverse_variance,
         resample_bank, psf_bank,
     )
     above = jnp.where(strip < strips - 1, above.astype(jnp.float32), 0.0)

time: 140 us -> 126 us (0.900)
  Pallas kernels: 129 us -> 109 us
  starting transfers between devices: 0 us -> 6.5 us
  local copies, waits for them, and re-layouts: 0 us -> 2.92 us
  other arithmetic: 9.89 us -> 7.18 us
    pallas_call x1, Pallas kernels: 129 us -> 109 us  [gradient_parts(): pl.pallas_call(functools.partial(forward_kernel, plan, per_dev), out_shap...]
    ppermute x0 -> x2, starting transfers between devices: none -> 6.5 us  [passed_along(): lax.ppermute(value, axis, [(source, source + steps) for source in range(i...]
    unnamed x0 -> x6, local copies, waits for them, and re-layouts: none -> 2.92 us
  transfers between devices with their start and end apart: 0 -> 2, of which waited for: 0 -> 1; matrix products, arithmetic and copies ran while one was open for 0% -> 0% of each run, Pallas kernels for 0% -> 0%
where the time goes in v3:
time: 126 us
  Pallas kernels  109 us (87%)
  other arithmetic  7.18 us (6%)
  starting transfers between devices  6.5 us (5%)
  local copies, waits for them, and re-layouts  2.92 us (2%)
    pallas_call x1, Pallas kernels, gradient_parts(): pl.pallas_call(functools.partial(forward_kernel, plan, per_dev), out_shap...  109 us
    ppermute x2, starting transfers between devices, passed_along(): lax.ppermute(value, axis, [(source, source + steps) for source in range(i...  6.5 us
    add x1, other arithmetic, on_device(): return middle + above + below  6.03 us
    unnamed x6, local copies, waits for them, and re-layouts  2.92 us
  transfers between devices with their start and end apart: 2, of which 1 were waited for; matrix products, arithmetic and copies ran while one was open for 0% of the time, Pallas kernels for 0%

profile of v3, /device:TPU:1, one launch (start us, length us, event | category | flops | bytes accessed | tf_op | source)
XLA Modules:
  0.0 126.2 jit_solution(15122474558249515304)
XLA Ops:
  0.0 0.8 select_reduce_fusion.2
  0.9 1.9 %collective-permute-start = (s32[128]{0:T(128)S(1)}, s32[128]{0:T(128)S(1)}, u32[]{:S(2)}, u32[]{:S(2)}) collective-permute-start(s32[128]{0:T(128)S(1)} %get-tuple-element.20), channel_id=1, source_target_pairs={{1,0},{2,1},{3,2},{4,3},{5,4},{6,5},{7,6},{9,8},{10,9},{11,10},{12... | collective-permute-start | bytes 1544 | tf_op jit(solution)/shard_map/ppermute | solution.py:28
  2.8 4.6 %collective-permute-start.1 = (s32[128]{0:T(128)S(1)}, s32[128]{0:T(128)S(1)}, u32[]{:S(2)}, u32[]{:S(2)}) collective-permute-start(s32[128]{0:T(128)S(1)} %get-tuple-element.21), channel_id=1, source_target_pairs={{0,1},{1,2},{2,3},{3,4},{4,5},{5,6},{6,7},{8,9},{9,10},{10,11},{11... | collective-permute-start | bytes 1544 | tf_op jit(solution)/shard_map/ppermute | solution.py:28
  7.4 0.2 select_reduce_fusion.1.prev_s
  7.6 0.1 select_reduce_fusion.last_s
  7.7 0.0 collective-permute-done
  7.7 0.4 collective-permute-done.1
  8.1 0.0 copy-start
  8.1 1.2 copy-done
  9.3 0.0 copy-start.1
  9.3 1.0 copy-done.1
  10.4 0.0 copy-start.2
  10.4 0.7 copy-done.2
  11.0 109.1 %gradient.1 = (f32[64,128,128]{2,1,0:T(8,128)}, bf16[64,128,128]{2,1,0:T(8,128)(2,1)S(1)}, bf16[64,128,128]{2,1,0:T(8,128)(2,1)}) custom-call(s32[128]{0:T(128)S(1)} %get-tuple-element.25.pos_s, s32[128]{0:T(128)S(1)} %get-tuple-element.22.own_s, s32[256]{0:T(256)S(1)} %pad_add_fusion.give_s, s32[128]{0:T(128)S(1)} %get-tuple-element.23.row_s, ...), custom_call_target="tpu_custom_call" | custom-call | tf_op jit(solution)/shard_map/gradient/pallas_call | solution.py:397
  120.2 6.0 %select_add_fusion = f32[64,128,128]{2,1,0:T(8,128)} fusion(bf16[64,128,128]{2,1,0:T(8,128)(2,1)} %get-tuple-element.10, f32[64,128,128]{2,1,0:T(8,128)} %get-tuple-element.8, bf16[64,128,128]{2,1,0:T(8,128)(2,1)S(1)} %get-tuple-element.9, pred[]{:T(512)S(6)} %gt.3, pred[]{:T(512)S(6)} %lt.70), kind=kLoop, calls=%fused_computation | loop fusion | flops 6291456 | bytes 12582914 | tf_op jit(solution)/shard_map/add | solution.py:480
  (4 shorter events, 0.1 us)
Async XLA Ops:
  0.9 6.8 %collective-permute-start = (s32[128]{0:T(128)S(1)}, s32[128]{0:T(128)S(1)}, u32[]{:S(2)}, u32[]{:S(2)}) collective-permute-start(s32[128]{0:T(128)S(1)} %get-tuple-element.20), channel_id=1, source_target_pairs={{1,0},{2,1},{3,2},{4,3},{5,4},{6,5},{7,6},{9,8},{10,9},{11,10},{12... | collective-permute-start | bytes 1544 | tf_op jit(solution)/shard_map/ppermute | solution.py:28
  2.8 5.3 %collective-permute-start.1 = (s32[128]{0:T(128)S(1)}, s32[128]{0:T(128)S(1)}, u32[]{:S(2)}, u32[]{:S(2)}) collective-permute-start(s32[128]{0:T(128)S(1)} %get-tuple-element.21), channel_id=1, source_target_pairs={{0,1},{1,2},{2,3},{3,4},{4,5},{5,6},{6,7},{8,9},{9,10},{10,11},{11... | collective-permute-start | bytes 1544 | tf_op jit(solution)/shard_map/ppermute | solution.py:28
  8.1 1.2 copy-start
  9.3 1.0 copy-start.1
  10.4 0.7 copy-start.2

commit v4 on v3

--- a/solution.py
+++ b/solution.py
@@ -10,7 +10,7 @@
 MESH = pl.DeviceIdType.MESH
 UNROLL = 4
 PIECES = 4
-VMEM_LIMIT = 50 * 1024 * 1024
+VMEM_LIMIT = 60 * 1024 * 1024
 
 
 def dot(a, b, dims):

time: 126 us -> 126 us (level)
  other arithmetic: 7.18 us -> 11 us
  local copies, waits for them, and re-layouts: 2.92 us -> 0.01 us
    unnamed x6 -> x2, local copies, waits for them, and re-layouts: 2.92 us -> 0.01 us
  transfers between devices with their start and end apart: 2 -> 2, of which waited for: 1 -> 0; matrix products, arithmetic and copies ran while one was open for 0% -> 1% of each run, Pallas kernels for 0% -> 0%
where the time goes in v4:
time: 126 us
  Pallas kernels  109 us (87%)
  other arithmetic  11 us (9%)
  starting transfers between devices  6.49 us (5%)
    pallas_call x1, Pallas kernels, gradient_parts(): pl.pallas_call(functools.partial(forward_kernel, plan, per_dev), out_shap...  109 us
    add x1, other arithmetic, on_device(): return middle + above + below  6.68 us
    ppermute x2, starting transfers between devices, passed_along(): lax.ppermute(value, axis, [(source, source + steps) for source in range(i...  6.49 us
  transfers between devices with their start and end apart: 2, of which 0 were waited for; matrix products, arithmetic and copies ran while one was open for 1% of the time, Pallas kernels for 0%

profile of v4, /device:TPU:1, one launch (start us, length us, event | category | flops | bytes accessed | tf_op | source)
XLA Modules:
  0.0 126.3 jit_solution(18107102005125311024)
XLA Ops:
  0.0 1.3 %select_reduce_fusion.2 = (s32[128]{0:T(128)}, s32[128]{0:T(128)S(1)}, s32[128]{0:T(128)S(1)}, pred[128,3]{0,1:T(4,128)(4,1)S(1)}) fusion(s32[128,6]{0,1:T(8,128)} %param.12, s32[]{:T(128)S(6)} %axis_index.25, s32[128,3]{0,1:T(4,128)} %param.11, s32[]{:T(128)S(6)} %axis_index.23), kind=kLoop, calls=%fused_computation.25 | loop fusion | flops 19584 | bytes 6536 | tf_op jit(solution)/shard_map/reduce_sum | solution.py:463
  1.3 0.5 broadcast_add_fusion
  1.9 0.0 copy-start
  1.9 0.5 compare_select_fusion
  2.3 1.9 %collective-permute-start = (s32[128]{0:T(128)S(1)}, s32[128]{0:T(128)S(1)}, u32[]{:S(2)}, u32[]{:S(2)}) collective-permute-start(s32[128]{0:T(128)S(1)} %get-tuple-element.20), channel_id=1, source_target_pairs={{1,0},{2,1},{3,2},{4,3},{5,4},{6,5},{7,6},{9,8},{10,9},{11,10},{12... | collective-permute-start | bytes 1544 | tf_op jit(solution)/shard_map/ppermute | solution.py:28
  4.3 4.6 %collective-permute-start.1 = (s32[128]{0:T(128)S(1)}, s32[128]{0:T(128)S(1)}, u32[]{:S(2)}, u32[]{:S(2)}) collective-permute-start(s32[128]{0:T(128)S(1)} %get-tuple-element.21), channel_id=1, source_target_pairs={{0,1},{1,2},{2,3},{3,4},{4,5},{5,6},{6,7},{8,9},{9,10},{10,11},{11... | collective-permute-start | bytes 1544 | tf_op jit(solution)/shard_map/ppermute | solution.py:28
  8.9 0.8 select_reduce_fusion.1.prev_s
  9.6 0.6 select_reduce_fusion.last_s
  10.3 0.0 collective-permute-done
  10.3 0.0 collective-permute-done.1
  10.3 0.6 pad_add_fusion.give_s
  10.8 0.0 copy-done
  10.8 108.7 %gradient.1 = (f32[64,128,128]{2,1,0:T(8,128)}, bf16[64,128,128]{2,1,0:T(8,128)(2,1)}, bf16[64,128,128]{2,1,0:T(8,128)(2,1)}) custom-call(s32[128]{0:T(128)} %copy-done, s32[128]{0:T(128)} %get-tuple-element.22.own_s, s32[256]{0:T(256)} %pad_add_fusion.give_s, s32[128]{0:T(128)} %get-tuple-element.23.row_s, s32[128]{0:T(128)} %get-tuple-element.11.col_s, ...), custom_call_target="tpu_custom_call" | custom-call | tf_op jit(solution)/shard_map/gradient/pallas_call | solution.py:397
  119.6 6.7 %select_add_fusion = f32[64,128,128]{2,1,0:T(8,128)} fusion(bf16[64,128,128]{2,1,0:T(8,128)(2,1)} %get-tuple-element.10, f32[64,128,128]{2,1,0:T(8,128)} %get-tuple-element.8, bf16[64,128,128]{2,1,0:T(8,128)(2,1)} %get-tuple-element.9, pred[]{:T(512)S(6)} %gt.3, pred[]{:T(512)S(6)} %lt.70), kind=kLoop, calls=%fused_computation | loop fusion | flops 6291456 | bytes 12582914 | tf_op jit(solution)/shard_map/add | solution.py:480
  (1 shorter events, 0.0 us)
Async XLA Ops:
  1.9 9.0 %copy-start = (s32[128]{0:T(128)}, s32[128]{0:T(128)S(1)}, u32[]{:S(2)}) copy-start(s32[128]{0:T(128)S(1)} %get-tuple-element.25.pos_s) | copy-start | bytes 1540
  2.3 7.9 %collective-permute-start = (s32[128]{0:T(128)S(1)}, s32[128]{0:T(128)S(1)}, u32[]{:S(2)}, u32[]{:S(2)}) collective-permute-start(s32[128]{0:T(128)S(1)} %get-tuple-element.20), channel_id=1, source_target_pairs={{1,0},{2,1},{3,2},{4,3},{5,4},{6,5},{7,6},{9,8},{10,9},{11,10},{12... | collective-permute-start | bytes 1544 | tf_op jit(solution)/shard_map/ppermute | solution.py:28
  4.3 6.0 %collective-permute-start.1 = (s32[128]{0:T(128)S(1)}, s32[128]{0:T(128)S(1)}, u32[]{:S(2)}, u32[]{:S(2)}) collective-permute-start(s32[128]{0:T(128)S(1)} %get-tuple-element.21), channel_id=1, source_target_pairs={{0,1},{1,2},{2,3},{3,4},{4,5},{5,6},{6,7},{8,9},{9,10},{10,11},{11... | collective-permute-start | bytes 1544 | tf_op jit(solution)/shard_map/ppermute | solution.py:28
